TPU v7x, 512 devices: a whole 4x8x8 slice. The times are simulated.
512 devices in a mesh: dp: 16 (over y, core), table: 32 (over x, z).
Axes of the slice: x: 4, y: 8, z: 8, core: 2. Of those that a mesh axis runs over, the one named last changes fastest.
Arguments:
- embedded: bfloat16 [2, 32768, 4096], P(None, 'dp', 'table'), may hold values from -1.1953125 to 1.1953125
- resid_grad: bfloat16 [2, 32768, 4096], P(None, 'dp', 'table'), may hold values from -0.29882812 to 0.29882812
- query_grad: bfloat16 [2, 32768, 2048], P(None, ('dp', 'table')), may hold values from -0.59765625 to 0.59765625
- query_weight: bfloat16 [4096, 2048], P('table'), may hold values from -0.09375 to 0.09375
- ngram_rows: int32 [2, 32768, 4], P(None, 'dp'), may hold values from 0 to 3199999, as said below
- touched_rows: int32 [32, 4, 12], replicated, may hold values from -1 to 3199999, as said below
- row_values: float32 [32, 4, 12, 1024], P('table'), may hold values from -6 to 6
- row_mean: float32 [32, 4, 12, 1024], P('table'), may hold values from -0.6 to 0.6
- row_square: float32 [32, 4, 12, 1024], P('table'), may hold values from 0.01 to 0.1
Outputs:
- weight_grad: float32 [4096, 2048], P('table')
- new_values: float32 [32, 4, 12, 1024], P('table')
- new_mean: float32 [32, 4, 12, 1024], P('table')
- new_square: float32 [32, 4, 12, 1024], P('table')
Inputs may be any that keep to these rules, and one draw needn't show every extreme that they name: `touched_rows`: owner o's list for slice s holds 1 to 12 distinct row ids of [o * 100000, (o + 1) * 100000) first, then -1; in every slice some owner's list is full. `ngram_rows`: every id of slice s is one of the listed rows of owner id // 100000 for slice s.
All inputs are finite; a program needn't handle non-finite values.
Results may differ from a plain program's by a relative error of at most 0.0003.
Values may be sent and summed in bfloat16 or wider, within the bound.
No kernel may reach another device: no remote copies, remote signals or barrier semaphores. Data moves between devices by JAX's collectives and lax.ppermute only.
A program may use at most 64 MiB of HBM per device.

v0:
```python
import jax
import jax.numpy as jnp
from jax import lax
from jax.sharding import Mesh, PartitionSpec as P

SW = 1024
beta_one = 0.9
beta_two = 0.95
learn_rate = 0.01
adam_eps = 1e-08
adam_step = 10
f32 = jnp.float32
bf16 = jnp.bfloat16


def adam_rows(grads, values, mean, square, live):
    corr_one = 1.0 - beta_one**adam_step
    corr_two = 1.0 - beta_two**adam_step
    mean_next = beta_one * mean + (1.0 - beta_one) * grads
    square_next = beta_two * square + (1.0 - beta_two) * grads * grads
    update = learn_rate * (mean_next / corr_one) / (jnp.sqrt(square_next / corr_two) + adam_eps)
    values_next = values - update
    return (
        jnp.where(live, values_next, values),
        jnp.where(live, mean_next, mean),
        jnp.where(live, square_next, square),
    )


def over_tokens(left, right):
    return lax.dot_general(left, right, (((0,), (0,)), ((), ())), preferred_element_type=f32)


def shift(array, axis, step):
    size = lax.axis_size(axis)
    return lax.ppermute(array, axis, [(i, (i + step) % size) for i in range(size)])


def local(
    embedded,
    resid_grad,
    query_grad,
    query_weight,
    ngram_rows,
    touched_rows,
    row_values,
    row_mean,
    row_square,
):
    micro, group, width = embedded.shape
    per, hidden = query_grad.shape[1:]
    nx, nz, ny = (lax.axis_size("x"), lax.axis_size("z"), lax.axis_size("y"))
    x_idx, z_idx, core = (lax.axis_index("x"), lax.axis_index("z"), lax.axis_index("core"))
    tables, slices, entries = touched_rows.shape
    part = hidden // nx
    tokens = micro * group
    groups = ny * 2
    rows_p = width // groups

    def token_order(array):
        tail = array.shape[2:]
        array = array.reshape((micro, nx, nz, per) + tail)
        return array.transpose((2, 1, 0, 3) + tuple(range(4, array.ndim))).reshape((tokens,) + tail)

    def by_part(array):
        return array.reshape(-1, nx, part).transpose(1, 0, 2)

    query = lax.all_to_all(by_part(query_grad), "x", 0, 0, tiled=True)
    query = lax.all_gather(query.reshape(nx * micro * per, part), "z", axis=0, tiled=True)
    weight = lax.all_to_all(by_part(query_weight), "x", 0, 0, tiled=True)
    emb = token_order(embedded)
    half = tokens // 2
    emb_back = shift(emb, "x", 1)
    emb_front = shift(emb, "x", -1)
    far_low = shift(emb_back[:half], "x", 1)
    far_high = shift(emb_front[half:], "x", -1)
    emb_far = jnp.concatenate([far_low, far_high], axis=0)
    emb_all = [emb, emb_front, emb_far, emb_back]
    ids = token_order(ngram_rows)
    lists = touched_rows.transpose(1, 2, 0).reshape(slices, entries * tables)

    def onehot(ids_of, list_of):
        return (ids_of[:, None] == list_of[None, :]).astype(bf16)

    own_ids = lax.dynamic_index_in_dim(ids, x_idx, 1, False)
    own_list = lax.dynamic_index_in_dim(lists, x_idx, 0, False)
    resid_rows = over_tokens(onehot(own_ids, own_list), token_order(resid_grad))
    row_parts = []
    for s in range(slices):
        seg = over_tokens(onehot(ids[:, s], lists[s]), query)
        high = lax.reduce_precision(seg, 8, 7)
        low = (seg - high).astype(bf16)
        one = lax.dot_general(
            high.astype(bf16), weight[s], (((1,), (1,)), ((), ())), preferred_element_type=f32
        )
        two = lax.dot_general(low, weight[s], (((1,), (1,)), ((), ())), preferred_element_type=f32)
        row_parts.append(one + two + jnp.where(x_idx == s, resid_rows, 0.0))
    row_sum = jnp.stack(row_parts).reshape(groups, slices * entries // groups * tables, width)
    w_parts = [over_tokens(piece, query) for piece in emb_all]
    w_sum = jnp.stack(w_parts)
    lanes = 128
    w_sum = w_sum.reshape(nx, groups, rows_p, part // lanes, lanes).transpose(1, 0, 3, 2, 4)
    w_sum = w_sum.reshape(groups, nx * part // lanes * rows_p, lanes)
    both = jnp.concatenate([w_sum, row_sum], axis=1)
    both = both.reshape(ny, 2, both.shape[1], lanes)
    first = core == 0
    send = jnp.where(first, both[:, 1], both[:, 0])
    keep = jnp.where(first, both[:, 0], both[:, 1])
    pair = keep + shift(send, "core", 1)
    pieces = lax.all_to_all(pair, "y", 0, 0, tiled=True)
    total = jnp.sum(pieces, axis=0)
    w_rows = nx * part // lanes * rows_p
    w_mine = total[:w_rows].reshape(nx, part // lanes * rows_p, lanes)
    twice = jnp.concatenate([w_mine, w_mine], axis=0)
    w_mine = lax.dynamic_slice_in_dim(twice, nx - x_idx, nx, 0)
    w_mine = lax.all_to_all(w_mine, "x", 0, 0, tiled=True).reshape(w_rows, lanes)
    pairs = slices * entries // groups
    r_mine = total[w_rows:].reshape(pairs, tables, width).transpose(1, 0, 2)
    r_mine = lax.all_to_all(r_mine, ("x", "z"), 0, 0, tiled=True)
    r_mine = jnp.sum(r_mine.reshape(nx, nz, pairs, width), axis=0)
    r_mine = r_mine.transpose(1, 0, 2).reshape(pairs * nz, lanes)
    piece = jnp.concatenate([w_mine, r_mine], axis=0)
    spread = jnp.broadcast_to(piece[None], (ny,) + piece.shape)
    mine = lax.all_to_all(spread, "y", 0, 0, tiled=True)
    other = shift(mine, "core", 1)
    full = jnp.stack([jnp.where(first, mine, other), jnp.where(first, other, mine)], axis=1)
    full = full.reshape((groups,) + piece.shape)
    weight_grad = full[:, :w_rows].reshape(groups, hidden // lanes, rows_p, lanes)
    weight_grad = weight_grad.transpose(0, 2, 1, 3).reshape(width, hidden)
    grads = full[:, w_rows:].reshape(slices, entries, nz * width)
    mine_rows = lax.dynamic_index_in_dim(touched_rows, x_idx * nz + z_idx, 0, False)
    live = (mine_rows >= 0)[..., None]
    values_next, mean_next, square_next = adam_rows(
        grads, row_values[0], row_mean[0], row_square[0], live
    )
    return (weight_grad, values_next[None], mean_next[None], square_next[None])


def solution(mesh):
    fine = Mesh(mesh.devices.reshape(8, 2, 4, 8), ("y", "core", "x", "z"))
    dp, table = (("y", "core"), ("x", "z"))
    placed = (
        P(None, dp, table),
        P(None, dp, table),
        P(None, dp + table, None),
        P(table, None),
        P(None, dp, None),
        P(),
        P(table, None, None, None),
        P(table, None, None, None),
        P(table, None, None, None),
    )
    return jax.shard_map(
        local,
        mesh=fine,
        in_specs=placed,
        out_specs=(
            P(table, None),
            P(table, None, None, None),
            P(table, None, None, None),
            P(table, None, None, None),
        ),
        check_vma=False,
    )
```

profile of v0, /device:TPU:1, one launch (start us, length us, event | category | flops | bytes accessed | tf_op | source)
XLA Modules:
  0.0 213.3 jit_solution(14318160484905589885)
XLA Ops:
  7.2 1.5 reshape.141
  8.9 11.7 %all_to_all.30 = bf16[4,128,512]{2,1,0:T(8,128)(2,1)S(1)} all-to-all(bf16[4,128,512]{2,1,0:T(8,128)(2,1)S(1)} %copy.185), channel_id=1, replica_groups=mesh['y'=8,'core'=2,'x'=4,'z'=8] {'x'}, dimensions={0} | all-to-all | bytes 1048576 | tf_op jit(solution)/shard_map/all_to_all | solution.py:68
  21.7 2.2 %collective-permute-start.1 = (bf16[4096,128]{1,0:T(8,128)(2,1)S(1)}, bf16[4096,128]{1,0:T(8,128)(2,1)}, u32[]{:S(2)}, u32[]{:S(2)}) collective-permute-start(bf16[4096,128]{1,0:T(8,128)(2,1)S(1)} %bitcast.145), channel_id=1, source_target_pairs={{0,8},{8,16},{16,24},{24,0},{1,9},{9,17},{17,25},{25,1},{2,10},{10... | collective-permute-start | bytes 3145736 | tf_op jit(solution)/shard_map/ppermute | solution.py:36
  23.9 4.3 %collective-permute-start = (bf16[4096,128]{1,0:T(8,128)(2,1)S(1)}, bf16[4096,128]{1,0:T(8,128)(2,1)}, u32[]{:S(2)}, u32[]{:S(2)}) collective-permute-start(bf16[4096,128]{1,0:T(8,128)(2,1)S(1)} %bitcast.146), channel_id=1, source_target_pairs={{0,24},{8,0},{16,8},{24,16},{1,25},{9,1},{17,9},{25,17},{2,26},{10... | collective-permute-start | bytes 3145736 | tf_op jit(solution)/shard_map/ppermute | solution.py:36
  28.3 2.0 copy.189
  30.3 3.5 %all-to-all-start.1 = ((bf16[4,128,512]{1,2,0:T(8,128)(2,1)}), bf16[4,128,512]{1,2,0:T(8,128)(2,1)S(1)}, u32[]{:S(2)}, u32[]{:S(2)}) async-start(bf16[4,128,512]{1,2,0:T(8,128)(2,1)} %bitcast.22), calls=%async_computation.1 | async-start | bytes 1048576 | tf_op jit(solution)/shard_map/all_to_all | solution.py:70
  35.7 1.3 copy.184
  37.1 3.7 %fusion = f32[384,128]{1,0:T(8,128)S(1)} fusion(bf16[4096,128]{1,0:T(8,128)(2,1)} %bitcast.152, s32[384]{0:T(512)S(1)} %dynamic-slice_reduce_fusion, s32[4096]{0:T(1024)S(1)} %bitcast.166), kind=kOutput, calls=%fused_computation.3 | convolution fusion | flops 404226048 | bytes 1263104 | tf_op jit(solution)/shard_map/dot_general | solution.py:31
  40.8 3.9 %collective-permute-done = bf16[4096,128]{1,0:T(8,128)(2,1)} collective-permute-done((bf16[4096,128]{1,0:T(8,128)(2,1)S(1)}, bf16[4096,128]{1,0:T(8,128)(2,1)}, u32[]{:S(2)}, u32[]{:S(2)}) %collective-permute-start) | collective-permute-done | bytes 1048608 | tf_op jit(solution)/shard_map/ppermute | solution.py:36
  45.8 5.4 %collective-permute-start.3 = (bf16[2048,128]{1,0:T(8,128)(2,1)S(1)}, bf16[2048,128]{1,0:T(8,128)(2,1)}, u32[]{:S(2)}, u32[]{:S(2)}) collective-permute-start(bf16[2048,128]{1,0:T(8,128)(2,1)S(1)} %slice.91), channel_id=1, source_target_pairs={{0,24},{8,0},{16,8},{24,16},{1,25},{9,1},{17,9},{25,17},{2,26},{10... | collective-permute-start | bytes 1572872 | tf_op jit(solution)/shard_map/ppermute | solution.py:36
  52.3 2.1 collective-permute-start.2
  54.4 31.0 %all-gather.2.cloned.1.call-done = bf16[4096,512]{0,1:T(8,128)(2,1)} async-done(((bf16[512,512]{0,1:T(8,128)(2,1)}), bf16[4096,512]{0,1:T(8,128)(2,1)}) %all-gather.2.cloned.1.call-update) | async-done | bytes 4194320 | tf_op jit(solution)/shard_map/all_gather | solution.py:69
  85.5 4.1 %convolution_bitcast_fusion.3 = f32[1,16,8,4,128]{4,2,3,1,0:T(8,128)S(1)} fusion(bf16[4,128,4096,1]{2,1,0,3:T(8,128)(2,1)} %bitcast.138, bf16[128,4096]{1,0:T(8,128)(2,1)} %copy.184), kind=kOutput, calls=%fused_computation.26 | convolution fusion | flops 536870912 | bytes 5505024 | tf_op jit(solution)/shard_map/dot_general | solution.py:31
  89.6 2.7 %convolution_bitcast_fusion = f32[1,16,8,4,128]{4,2,3,1,0:T(8,128)S(1)} fusion(bf16[4096,128]{1,0:T(8,128)(2,1)} %collective-permute-done.1, bf16[4096,512]{0,1:T(8,128)(2,1)S(1)} %copy-done), kind=kOutput, calls=%fused_computation.23 | convolution fusion | flops 536870912 | bytes 5505024 | tf_op jit(solution)/shard_map/dot_general | solution.py:31
  92.4 2.7 %convolution_bitcast_fusion.2 = f32[1,16,8,4,128]{4,2,3,1,0:T(8,128)S(1)} fusion(bf16[4096,128]{1,0:T(8,128)(2,1)} %collective-permute-done, bf16[4096,512]{0,1:T(8,128)(2,1)S(1)} %copy-done), kind=kOutput, calls=%fused_computation.25 | convolution fusion | flops 536870912 | bytes 5505024 | tf_op jit(solution)/shard_map/dot_general | solution.py:31
  95.1 2.6 %convolution_bitcast_fusion.1 = f32[1,16,8,4,128]{4,2,3,1,0:T(8,128)S(1)} fusion(bf16[4096,512]{0,1:T(8,128)(2,1)S(1)} %copy-done, bf16[2048,128]{1,0:T(8,128)(2,1)} %collective-permute-done.3, bf16[2048,128]{1,0:T(8,128)(2,1)S(1)} %collective-permute-done.2), kind=kOutput, calls=%fused_computation.24 | convolution fusion | flops 538968064 | bytes 5505024 | tf_op jit(solution)/shard_map/dot_general | solution.py:31
  97.9 2.5 %fusion.5 = f32[384,512]{1,0:T(8,128)S(1)} fusion(bf16[4096,512]{0,1:T(8,128)(2,1)S(1)} %copy-done, s32[384]{0:T(512)S(1)} %eq.126, s32[4096]{0:T(1024)S(1)} %bitcast.165), kind=kOutput, calls=%fused_computation.9 | convolution fusion | flops 1613758464 | bytes 4998656 | tf_op jit(solution)/shard_map/dot_general | solution.py:31
  100.6 4.8 %fusion.4 = f32[384,512]{1,0:T(8,128)S(1)} fusion(bf16[4096,512]{0,1:T(8,128)(2,1)} %all-gather.2.cloned.1.call-done, s32[384]{0:T(512)S(1)} %eq.120, s32[4096]{0:T(1024)S(1)} %bitcast.164), kind=kOutput, calls=%fused_computation.8 | convolution fusion | flops 1613758464 | bytes 4998656 | tf_op jit(solution)/shard_map/dot_general | solution.py:31
  105.7 2.5 %fusion.3 = f32[384,512]{1,0:T(8,128)S(1)} fusion(bf16[4096,512]{0,1:T(8,128)(2,1)S(1)} %copy-done.1, s32[384]{0:T(512)S(1)} %eq.114, s32[4096]{0:T(1024)S(1)} %bitcast.163), kind=kOutput, calls=%fused_computation.7 | convolution fusion | flops 1613758464 | bytes 4998656 | tf_op jit(solution)/shard_map/dot_general | solution.py:31
  108.5 2.7 %fusion.2 = f32[384,512]{1,0:T(8,128)S(1)} fusion(bf16[4096,512]{0,1:T(8,128)(2,1)S(1)} %copy-done.1, s32[384]{0:T(512)S(1)} %eq.103, s32[4096]{0:T(1024)S(1)} %bitcast.162), kind=kOutput, calls=%fused_computation.6 | convolution fusion | flops 1613758464 | bytes 4998656 | tf_op jit(solution)/shard_map/dot_general | solution.py:31
  112.8 2.7 %collective-permute-start.4 = (f32[8,224,128]{2,1,0:T(8,128)S(1)}, f32[8,224,128]{2,1,0:T(8,128)S(1)}, u32[]{:S(2)}, u32[]{:S(2)}) collective-permute-start(f32[8,224,128]{2,1,0:T(8,128)S(1)} %select_bitcast_fusion), channel_id=1, source_target_pairs={{0,32},{32,0},{1,33},{33,1},{2,34},{34,2},{3,35},{35,3},{4,36},{36... | collective-permute-start | bytes 2752520 | tf_op jit(solution)/shard_map/ppermute | solution.py:36
  115.5 2.1 collective-permute-done.4
  117.6 1.1 fusion.30
  118.7 6.5 %all-to-all-start.2 = ((f32[8,224,128]{2,1,0:T(8,128)}), f32[8,224,128]{2,1,0:T(8,128)S(1)}, u32[]{:S(2)}, u32[]{:S(2)}) async-start(f32[8,224,128]{2,1,0:T(8,128)} %fusion.30), calls=%async_computation.2 | async-start | bytes 1835008 | tf_op jit(solution)/shard_map/all_to_all | solution.py:110
  125.2 26.4 %all-to-all-done.2 = f32[8,224,128]{2,1,0:T(8,128)S(1)} async-done(((f32[8,224,128]{2,1,0:T(8,128)}), f32[8,224,128]{2,1,0:T(8,128)S(1)}, u32[]{:S(2)}, u32[]{:S(2)}) %all-to-all-start.2) | async-done | bytes 917536 | tf_op jit(solution)/shard_map/all_to_all | solution.py:110
  152.3 6.6 %all-to-all-start.4 = ((f32[32,3,128]{2,1,0:T(4,128)}), f32[32,3,128]{2,1,0:T(4,128)S(1)}, u32[]{:S(2)}, u32[]{:S(2)}) async-start(f32[32,3,128]{2,1,0:T(4,128)} %copy.200), calls=%async_computation.4 | async-start | bytes 131072 | tf_op jit(solution)/shard_map/all_to_all | solution.py:119
  159.6 8.2 %all-to-all-done.4 = f32[32,3,128]{2,1,0:T(4,128)S(1)} async-done(((f32[32,3,128]{2,1,0:T(4,128)}), f32[32,3,128]{2,1,0:T(4,128)S(1)}, u32[]{:S(2)}, u32[]{:S(2)}) %all-to-all-start.4) | async-done | bytes 49184 | tf_op jit(solution)/shard_map/all_to_all | solution.py:119
  167.8 3.3 %all-to-all-start.3 = ((f32[4,32,128]{2,1,0:T(8,128)}), f32[4,32,128]{2,1,0:T(8,128)S(1)}, u32[]{:S(2)}, u32[]{:S(2)}) async-start(f32[4,32,128]{2,1,0:T(8,128)} %fusion.45), calls=%async_computation.3 | async-start | bytes 131072 | tf_op jit(solution)/shard_map/all_to_all | solution.py:116
  171.1 4.4 %all-to-all-done.3 = f32[4,32,128]{2,1,0:T(8,128)S(1)} async-done(((f32[4,32,128]{2,1,0:T(8,128)}), f32[4,32,128]{2,1,0:T(8,128)S(1)}, u32[]{:S(2)}, u32[]{:S(2)}) %all-to-all-start.3) | async-done | bytes 65568 | tf_op jit(solution)/shard_map/all_to_all | solution.py:116
  175.6 18.7 %all_to_all.31 = f32[8,152,128]{2,1,0:T(8,128)S(1)} all-to-all(f32[8,152,128]{2,1,0:T(8,128)S(1)} %broadcast_in_dim.34), channel_id=1, replica_groups=mesh['y'=8,'core'=2,'x'=4,'z'=8] {'y'}, dimensions={0} | all-to-all | bytes 1245184 | tf_op jit(solution)/shard_map/all_to_all | solution.py:124
  194.3 6.2 %collective-permute-start.5 = (f32[8,152,128]{2,1,0:T(8,128)S(1)}, f32[8,152,128]{2,1,0:T(8,128)S(1)}, u32[]{:S(2)}, u32[]{:S(2)}) collective-permute-start(f32[8,152,128]{2,1,0:T(8,128)S(1)} %all_to_all.31), channel_id=1, source_target_pairs={{0,32},{32,0},{1,33},{33,1},{2,34},{34,2},{3,35},{35,3},{4,36},{36... | collective-permute-start | bytes 1867784 | tf_op jit(solution)/shard_map/ppermute | solution.py:36
  200.8 1.4 collective-permute-done.5
  (75 shorter events, 13.8 us)
Async XLA Ops:
  7.2 14.5 %copy-start.2 = (bf16[2,2048,128]{2,1,0:T(8,128)(2,1)S(1)}, bf16[2,2048,128]{2,1,0:T(8,128)(2,1)}, u32[]{:S(2)}) copy-start(bf16[2,2048,128]{2,1,0:T(8,128)(2,1)} %param.9) | copy-start | bytes 3145732
  7.2 78.3 %all-gather.2.cloned.1.call-start = ((), (), s32[]{:S(2)}) async-start(), calls=%async_computation.6 | async-start | bytes 4718592 | tf_op jit(solution)/shard_map/all_gather | solution.py:69
  8.7 25.1 %copy-start.4 = (s32[32,4,12]{0,1,2:T(4,128)S(1)}, s32[32,4,12]{0,1,2:T(4,128)}, u32[]{:S(2)}) copy-start(s32[32,4,12]{0,1,2:T(4,128)} %param.14) | copy-start | bytes 18436
  8.7 25.2 %copy-start.8 = (s32[2,2048,4]{1,2,0:T(4,128)S(1)}, s32[2,2048,4]{1,2,0:T(4,128)}, u32[]{:S(2)}) copy-start(s32[2,2048,4]{1,2,0:T(4,128)} %param.13) | copy-start | bytes 196612
  8.8 25.6 %copy-start.3 = (bf16[2,2048,128]{2,1,0:T(8,128)(2,1)S(1)}, bf16[2,2048,128]{2,1,0:T(8,128)(2,1)}, u32[]{:S(2)}) copy-start(bf16[2,2048,128]{2,1,0:T(8,128)(2,1)} %param.10) | copy-start | bytes 3145732
  21.7 29.5 %collective-permute-start.1 = (bf16[4096,128]{1,0:T(8,128)(2,1)S(1)}, bf16[4096,128]{1,0:T(8,128)(2,1)}, u32[]{:S(2)}, u32[]{:S(2)}) collective-permute-start(bf16[4096,128]{1,0:T(8,128)(2,1)S(1)} %bitcast.145), channel_id=1, source_target_pairs={{0,8},{8,16},{16,24},{24,0},{1,9},{9,17},{17,25},{25,1},{2,10},{10... | collective-permute-start | bytes 3145736 | tf_op jit(solution)/shard_map/ppermute | solution.py:36
  23.9 20.8 %collective-permute-start = (bf16[4096,128]{1,0:T(8,128)(2,1)S(1)}, bf16[4096,128]{1,0:T(8,128)(2,1)}, u32[]{:S(2)}, u32[]{:S(2)}) collective-permute-start(bf16[4096,128]{1,0:T(8,128)(2,1)S(1)} %bitcast.146), channel_id=1, source_target_pairs={{0,24},{8,0},{16,8},{24,16},{1,25},{9,1},{17,9},{25,17},{2,26},{10... | collective-permute-start | bytes 3145736 | tf_op jit(solution)/shard_map/ppermute | solution.py:36
  30.3 70.1 %all-to-all-start.1 = ((bf16[4,128,512]{1,2,0:T(8,128)(2,1)}), bf16[4,128,512]{1,2,0:T(8,128)(2,1)S(1)}, u32[]{:S(2)}, u32[]{:S(2)}) async-start(bf16[4,128,512]{1,2,0:T(8,128)(2,1)} %bitcast.22), calls=%async_computation.1 | async-start | bytes 1048576 | tf_op jit(solution)/shard_map/all_to_all | solution.py:70
  45.8 49.3 %collective-permute-start.3 = (bf16[2048,128]{1,0:T(8,128)(2,1)S(1)}, bf16[2048,128]{1,0:T(8,128)(2,1)}, u32[]{:S(2)}, u32[]{:S(2)}) collective-permute-start(bf16[2048,128]{1,0:T(8,128)(2,1)S(1)} %slice.91), channel_id=1, source_target_pairs={{0,24},{8,0},{16,8},{24,16},{1,25},{9,1},{17,9},{25,17},{2,26},{10... | collective-permute-start | bytes 1572872 | tf_op jit(solution)/shard_map/ppermute | solution.py:36
  52.3 42.8 %collective-permute-start.2 = (bf16[2048,128]{1,0:T(8,128)(2,1)S(1)}, bf16[2048,128]{1,0:T(8,128)(2,1)S(1)}, u32[]{:S(2)}, u32[]{:S(2)}) collective-permute-start(bf16[2048,128]{1,0:T(8,128)(2,1)S(1)} %slice.90), channel_id=1, source_target_pairs={{0,8},{8,16},{16,24},{24,0},{1,9},{9,17},{17,25},{25,1},{2,10},{10... | collective-permute-start | bytes 1572872 | tf_op jit(solution)/shard_map/ppermute | solution.py:36
  85.5 4.2 %copy-start = (bf16[4096,512]{0,1:T(8,128)(2,1)S(1)}, bf16[4096,512]{0,1:T(8,128)(2,1)}, u32[]{:S(2)}) copy-start(bf16[4096,512]{0,1:T(8,128)(2,1)} %all-gather.2.cloned.1.call-done) | copy-start | bytes 12582916
  100.6 5.1 %copy-start.1 = (bf16[4096,512]{0,1:T(8,128)(2,1)S(1)}, bf16[4096,512]{0,1:T(8,128)(2,1)}, u32[]{:S(2)}) copy-start(bf16[4096,512]{0,1:T(8,128)(2,1)} %all-gather.2.cloned.1.call-done) | copy-start | bytes 12582916
  112.8 4.8 %collective-permute-start.4 = (f32[8,224,128]{2,1,0:T(8,128)S(1)}, f32[8,224,128]{2,1,0:T(8,128)S(1)}, u32[]{:S(2)}, u32[]{:S(2)}) collective-permute-start(f32[8,224,128]{2,1,0:T(8,128)S(1)} %select_bitcast_fusion), channel_id=1, source_target_pairs={{0,32},{32,0},{1,33},{33,1},{2,34},{34,2},{3,35},{35,3},{4,36},{36... | collective-permute-start | bytes 2752520 | tf_op jit(solution)/shard_map/ppermute | solution.py:36
  118.7 32.9 %all-to-all-start.2 = ((f32[8,224,128]{2,1,0:T(8,128)}), f32[8,224,128]{2,1,0:T(8,128)S(1)}, u32[]{:S(2)}, u32[]{:S(2)}) async-start(f32[8,224,128]{2,1,0:T(8,128)} %fusion.30), calls=%async_computation.2 | async-start | bytes 1835008 | tf_op jit(solution)/shard_map/all_to_all | solution.py:110
  152.3 15.5 %all-to-all-start.4 = ((f32[32,3,128]{2,1,0:T(4,128)}), f32[32,3,128]{2,1,0:T(4,128)S(1)}, u32[]{:S(2)}, u32[]{:S(2)}) async-start(f32[32,3,128]{2,1,0:T(4,128)} %copy.200), calls=%async_computation.4 | async-start | bytes 131072 | tf_op jit(solution)/shard_map/all_to_all | solution.py:119
  167.8 7.7 %all-to-all-start.3 = ((f32[4,32,128]{2,1,0:T(8,128)}), f32[4,32,128]{2,1,0:T(8,128)S(1)}, u32[]{:S(2)}, u32[]{:S(2)}) async-start(f32[4,32,128]{2,1,0:T(8,128)} %fusion.45), calls=%async_computation.3 | async-start | bytes 131072 | tf_op jit(solution)/shard_map/all_to_all | solution.py:116
  194.3 9.2 %copy-start.5 = (f32[1,4,12,1024]{3,1,2,0:T(4,128)S(1)}, f32[1,4,12,1024]{3,1,2,0:T(4,128)}, u32[]{:S(2)}) copy-start(f32[1,4,12,1024]{3,1,2,0:T(4,128)} %param.17) | copy-start | bytes 589828
  194.3 9.2 %copy-start.6 = (f32[1,4,12,1024]{3,1,2,0:T(4,128)S(1)}, f32[1,4,12,1024]{3,1,2,0:T(4,128)}, u32[]{:S(2)}) copy-start(f32[1,4,12,1024]{3,1,2,0:T(4,128)} %param.16) | copy-start | bytes 589828
  194.3 9.2 %copy-start.7 = (f32[1,4,12,1024]{3,1,2,0:T(4,128)S(1)}, f32[1,4,12,1024]{3,1,2,0:T(4,128)}, u32[]{:S(2)}) copy-start(f32[1,4,12,1024]{3,1,2,0:T(4,128)} %param.15) | copy-start | bytes 589828
  194.3 7.9 %collective-permute-start.5 = (f32[8,152,128]{2,1,0:T(8,128)S(1)}, f32[8,152,128]{2,1,0:T(8,128)S(1)}, u32[]{:S(2)}, u32[]{:S(2)}) collective-permute-start(f32[8,152,128]{2,1,0:T(8,128)S(1)} %all_to_all.31), channel_id=1, source_target_pairs={{0,32},{32,0},{1,33},{33,1},{2,34},{34,2},{3,35},{35,3},{4,36},{36... | collective-permute-start | bytes 1867784 | tf_op jit(solution)/shard_map/ppermute | solution.py:36
Sparse Core Ops, SparseCore 0:
  21.8 63.6 all-gather.1
where the time goes:
time: 214 us; the launch traced here: 213 us
  waiting for transfers between devices  77.4 us (36%)
  starting transfers between devices  42.9 us (20%)
  blocking collectives  30.4 us (14%)
  matrix products  30.4 us (14%)
  local copies, waits for them, and re-layouts  14.8 us (7%)
  between operations  14.5 us (7%)
  other arithmetic  2.73 us (1%)
    all_gather x1, waiting for transfers between devices, local(): lax.all_gather(query.reshape(nx * micro * per, part), 'z', axis=0, tiled=...  31 us
    dot_general x9, matrix products, over_tokens(): lax.dot_general(left, right, (((0,), (0,)), ((), ())), preferred_element_...  28.3 us
    all_to_all x1, waiting for transfers between devices, local(): pieces = lax.all_to_all(pair, 'y', 0, 0, tiled=True)  26.4 us
    ppermute x6, starting transfers between devices, shift(): lax.ppermute(array, axis, [(i, (i + step) % size) for i in range(size)])  23 us
    all_to_all x1, blocking collectives, local(): mine = lax.all_to_all(spread, 'y', 0, 0, tiled=True)  18.7 us
    all_to_all x1, blocking collectives, local(): query = lax.all_to_all(by_part(query_grad), 'x', 0, 0, tiled=True)  11.7 us
    all_to_all x1, waiting for transfers between devices, local(): r_mine = lax.all_to_all(r_mine, ('x', 'z'), 0, 0, tiled=True)  8.21 us
    ppermute x6, waiting for transfers between devices, shift(): lax.ppermute(array, axis, [(i, (i + step) % size) for i in range(size)])  7.41 us
  transfers between devices with their start and end apart: 11, of which 7 were waited for; matrix products, arithmetic and copies ran while one was open for 13% of the time, Pallas kernels for 0%

commit v1 on v0

--- a/solution.py
+++ b/solution.py
@@ -11,6 +11,12 @@
 adam_step = 10
 f32 = jnp.float32
 bf16 = jnp.bfloat16
+unit_connect = lambda u_in, d0: jnp.concatenate(
+    lax.all_to_all(
+        jnp.stack(lax.axis_size("z") * [u_in]), axis_name="z", split_axis=0, concat_axis=0
+    ),
+    axis=d0,
+)
 
 
 def adam_rows(grads, values, mean, square, live):
@@ -66,7 +72,7 @@
         return array.reshape(-1, nx, part).transpose(1, 0, 2)
 
     query = lax.all_to_all(by_part(query_grad), "x", 0, 0, tiled=True)
-    query = lax.all_gather(query.reshape(nx * micro * per, part), "z", axis=0, tiled=True)
+    query = unit_connect(query.reshape(nx * micro * per, part), 0)
     weight = lax.all_to_all(by_part(query_weight), "x", 0, 0, tiled=True)
     emb = token_order(embedded)
     half = tokens // 2

time: 214 us -> 263 us (1.23)
  waiting for transfers between devices: 77.4 us -> 111 us
  local copies, waits for them, and re-layouts: 14.8 us -> 35.3 us
  between operations: 14.5 us -> 1.16 us
  starting transfers between devices: 42.9 us -> 50.2 us
    all_to_all x0 -> x1, waiting for transfers between devices: none -> 50 us  [lax.all_to_all(jnp.stack(lax.axis_size('z') * [u_in]), axis_name='z', spl...]
    all_gather x1 -> x0, waiting for transfers between devices: 31 us -> none  [local(): lax.all_gather(query.reshape(nx * micro * per, part), 'z', axis=0, tiled=...]
    ppermute x6, waiting for transfers between devices: 7.41 us -> 22.5 us  [shift(): lax.ppermute(array, axis, [(i, (i + step) % size) for i in range(size)])]
    all_to_all x0 -> x1, starting transfers between devices: none -> 11.9 us  [lax.all_to_all(jnp.stack(lax.axis_size('z') * [u_in]), axis_name='z', spl...]
    dot_general x1 -> x5, local copies, waits for them, and re-layouts: 1.31 us -> 11 us  [over_tokens(): lax.dot_general(left, right, (((0,), (0,)), ((), ())), preferred_element_...]
    all_to_all x0 -> x1, local copies, waits for them, and re-layouts: none -> 6.53 us  [lax.all_to_all(jnp.stack(lax.axis_size('z') * [u_in]), axis_name='z', spl...]
    dot_general x9, matrix products: 28.3 us -> 24.7 us  [over_tokens(): lax.dot_general(left, right, (((0,), (0,)), ((), ())), preferred_element_...]
    ppermute x6, starting transfers between devices: 23 us -> 19.9 us  [shift(): lax.ppermute(array, axis, [(i, (i + step) % size) for i in range(size)])]
  transfers between devices with their start and end apart: 11 -> 11, of which waited for: 7 -> 7; matrix products, arithmetic and copies ran while one was open for 13% -> 20% of each run, Pallas kernels for 0% -> 0%
where the time goes in v1:
time: 263 us; the launch traced here: 261 us
  waiting for transfers between devices  111 us (42%)
  starting transfers between devices  50.2 us (19%)
  local copies, waits for them, and re-layouts  35.3 us (13%)
  blocking collectives  30.3 us (12%)
  matrix products  29.2 us (11%)
  other arithmetic  3.96 us (2%)
    all_to_all x1, waiting for transfers between devices, lax.all_to_all(jnp.stack(lax.axis_size('z') * [u_in]), axis_name='z', spl...  50 us
    all_to_all x1, waiting for transfers between devices, local(): pieces = lax.all_to_all(pair, 'y', 0, 0, tiled=True)  26.4 us
    dot_general x9, matrix products, over_tokens(): lax.dot_general(left, right, (((0,), (0,)), ((), ())), preferred_element_...  24.7 us
    ppermute x6, waiting for transfers between devices, shift(): lax.ppermute(array, axis, [(i, (i + step) % size) for i in range(size)])  22.5 us
    ppermute x6, starting transfers between devices, shift(): lax.ppermute(array, axis, [(i, (i + step) % size) for i in range(size)])  19.9 us
    all_to_all x1, blocking collectives, local(): mine = lax.all_to_all(spread, 'y', 0, 0, tiled=True)  18.7 us
    all_to_all x1, starting transfers between devices, lax.all_to_all(jnp.stack(lax.axis_size('z') * [u_in]), axis_name='z', spl...  11.9 us
    all_to_all x1, blocking collectives, local(): query = lax.all_to_all(by_part(query_grad), 'x', 0, 0, tiled=True)  11.6 us
  transfers between devices with their start and end apart: 11, of which 7 were waited for; matrix products, arithmetic and copies ran while one was open for 20% of the time, Pallas kernels for 0%

profile of v1, /device:TPU:1, one launch (start us, length us, event | category | flops | bytes accessed | tf_op | source)
XLA Modules:
  0.0 261.5 jit_solution(13330926334087371776)
XLA Ops:
  2.2 11.6 %all_to_all.35 = bf16[4,128,512]{2,1,0:T(8,128)(2,1)S(1)} all-to-all(bf16[4,128,512]{2,1,0:T(8,128)(2,1)S(1)} %copy.211), channel_id=1, replica_groups=mesh['y'=8,'core'=2,'x'=4,'z'=8] {'x'}, dimensions={0} | all-to-all | bytes 1048576 | tf_op jit(solution)/shard_map/all_to_all | solution.py:74
  13.9 2.3 stack.34
  16.3 11.9 %all-to-all-start.1 = ((bf16[8,512,512]{1,2,0:T(8,128)(2,1)}), bf16[8,512,512]{1,2,0:T(8,128)(2,1)}, u32[]{:S(2)}, u32[]{:S(2)}) async-start(bf16[8,512,512]{1,2,0:T(8,128)(2,1)} %stack.34), calls=%async_computation.1 | async-start | bytes 8388608 | tf_op jit(solution)/shard_map/all_to_all | solution.py:15
  28.2 2.8 %collective-permute-start = (bf16[4096,128]{1,0:T(8,128)(2,1)S(1)}, bf16[4096,128]{1,0:T(8,128)(2,1)S(1)}, u32[]{:S(2)}, u32[]{:S(2)}) collective-permute-start(bf16[4096,128]{1,0:T(8,128)(2,1)S(1)} %bitcast.177), channel_id=1, source_target_pairs={{0,24},{8,0},{16,8},{24,16},{1,25},{9,1},{17,9},{25,17},{2,26},{10... | collective-permute-start | bytes 3145736 | tf_op jit(solution)/shard_map/ppermute | solution.py:42
  31.0 2.5 collective-permute-start.1
  33.9 18.9 %collective-permute-done = bf16[4096,128]{1,0:T(8,128)(2,1)S(1)} collective-permute-done((bf16[4096,128]{1,0:T(8,128)(2,1)S(1)}, bf16[4096,128]{1,0:T(8,128)(2,1)S(1)}, u32[]{:S(2)}, u32[]{:S(2)}) %collective-permute-start) | collective-permute-done | bytes 1048608 | tf_op jit(solution)/shard_map/ppermute | solution.py:42
  53.7 4.0 %collective-permute-start.3 = (bf16[2048,128]{1,0:T(8,128)(2,1)}, bf16[2048,128]{1,0:T(8,128)(2,1)}, u32[]{:S(2)}, u32[]{:S(2)}) collective-permute-start(bf16[2048,128]{1,0:T(8,128)(2,1)} %slice.91), channel_id=1, source_target_pairs={{0,24},{8,0},{16,8},{24,16},{1,25},{9,1},{17,9},{25,17},{2,26},{10... | collective-permute-start | bytes 1572872 | tf_op jit(solution)/shard_map/ppermute | solution.py:42
  58.6 1.9 collective-permute-start.2
  60.7 2.1 copy.220
  62.8 2.3 copy.223
  66.8 3.7 %fusion.6 = f32[384,128]{1,0:T(8,128)S(1)} fusion(bf16[4096,128]{1,0:T(8,128)(2,1)} %bitcast.186, s32[384]{0:T(512)S(1)} %dynamic-slice_reduce_fusion, s32[4096]{0:T(1024)S(1)} %bitcast.200), kind=kOutput, calls=%fused_computation.6 | convolution fusion | flops 404226048 | bytes 1263104 | tf_op jit(solution)/shard_map/dot_general | solution.py:37
  74.9 50.0 %all-to-all-done.1 = bf16[8,512,512]{1,2,0:T(8,128)(2,1)} async-done(((bf16[8,512,512]{1,2,0:T(8,128)(2,1)}), bf16[8,512,512]{1,2,0:T(8,128)(2,1)}, u32[]{:S(2)}, u32[]{:S(2)}) %all-to-all-start.1) | async-done | bytes 4194336 | tf_op jit(solution)/shard_map/all_to_all | solution.py:15
  124.9 3.5 %all-to-all-start.2 = ((bf16[4,128,512]{1,2,0:T(8,128)(2,1)}), bf16[4,128,512]{1,2,0:T(8,128)(2,1)S(1)}, u32[]{:S(2)}, u32[]{:S(2)}) async-start(bf16[4,128,512]{1,2,0:T(8,128)(2,1)} %bitcast.36), calls=%async_computation.2 | async-start | bytes 1048576 | tf_op jit(solution)/shard_map/all_to_all | solution.py:76
  128.4 6.5 %copy.213 = bf16[8,512,512]{2,1,0:T(8,128)(2,1)} copy(bf16[8,512,512]{1,2,0:T(8,128)(2,1)} %all-to-all-done.1) | data formatting | bytes 8388608 | tf_op jit(solution)/shard_map/all_to_all | solution.py:15
  134.9 6.5 %copy.214 = bf16[512,4096]{1,0:T(8,128)(2,1)} copy(bf16[512,4096]{0,1:T(8,128)(2,1)} %bitcast.162) | data formatting | bytes 8388608 | tf_op jit(solution)/shard_map/dot_general | solution.py:37
  141.5 3.8 %convolution_bitcast_fusion = f32[1,16,8,4,128]{4,2,3,1,0:T(8,128)S(1)} fusion(bf16[4,128,4096,1]{2,1,0,3:T(8,128)(2,1)} %bitcast.173, bf16[128,4096]{1,0:T(8,128)(2,1)S(1)} %copy-done.6), kind=kOutput, calls=%fused_computation.23 | convolution fusion | flops 536870912 | bytes 5505024 | tf_op jit(solution)/shard_map/dot_general | solution.py:37
  150.0 2.0 copy-done
  152.0 3.6 %fusion = f32[384,512]{1,0:T(8,128)} fusion(bf16[4096,512]{1,0:T(8,128)(2,1)S(1)} %bitcast.163, s32[384]{0:T(512)S(1)} %eq.126, s32[4096]{0:T(1024)S(1)} %bitcast.199), kind=kOutput, calls=%fused_computation | convolution fusion | flops 1612185600 | bytes 4998656 | tf_op jit(solution)/shard_map/dot_general | solution.py:37
  155.6 3.6 %fusion.2 = f32[384,512]{1,0:T(8,128)} fusion(bf16[4096,512]{1,0:T(8,128)(2,1)S(1)} %bitcast.164, s32[384]{0:T(512)S(1)} %eq.120, s32[4096]{0:T(1024)S(1)} %bitcast.198), kind=kOutput, calls=%fused_computation.2 | convolution fusion | flops 1612185600 | bytes 4998656 | tf_op jit(solution)/shard_map/dot_general | solution.py:37
  159.2 2.7 %fusion.4 = f32[384,512]{1,0:T(8,128)S(1)} fusion(bf16[4096,512]{1,0:T(8,128)(2,1)S(1)} %bitcast.165, s32[384]{0:T(512)S(1)} %eq.114, s32[4096]{0:T(1024)S(1)} %bitcast.197), kind=kOutput, calls=%fused_computation.4 | convolution fusion | flops 1612185600 | bytes 4998656 | tf_op jit(solution)/shard_map/dot_general | solution.py:37
  161.9 2.9 %fusion.8 = f32[384,512]{1,0:T(8,128)S(1)} fusion(bf16[4096,512]{1,0:T(8,128)(2,1)S(1)} %bitcast.166, s32[384]{0:T(512)S(1)} %eq.103, s32[4096]{0:T(1024)S(1)} %bitcast.196), kind=kOutput, calls=%fused_computation.8 | convolution fusion | flops 1612185600 | bytes 4998656 | tf_op jit(solution)/shard_map/dot_general | solution.py:37
  164.8 1.5 fusion.46
  169.5 2.4 collective-permute-start.4
  172.0 2.1 collective-permute-done.4
  175.1 6.8 %all-to-all-start.3 = ((f32[8,224,128]{2,1,0:T(8,128)}), f32[8,224,128]{2,1,0:T(8,128)S(1)}, u32[]{:S(2)}, u32[]{:S(2)}) async-start(f32[8,224,128]{2,1,0:T(8,128)} %fusion.34), calls=%async_computation.3 | async-start | bytes 1835008 | tf_op jit(solution)/shard_map/all_to_all | solution.py:116
  182.0 26.4 %all-to-all-done.3 = f32[8,224,128]{2,1,0:T(8,128)S(1)} async-done(((f32[8,224,128]{2,1,0:T(8,128)}), f32[8,224,128]{2,1,0:T(8,128)S(1)}, u32[]{:S(2)}, u32[]{:S(2)}) %all-to-all-start.3) | async-done | bytes 917536 | tf_op jit(solution)/shard_map/all_to_all | solution.py:116
  209.1 4.9 %all-to-all-start.5 = ((f32[32,3,128]{2,1,0:T(4,128)}), f32[32,3,128]{2,1,0:T(4,128)S(1)}, u32[]{:S(2)}, u32[]{:S(2)}) async-start(f32[32,3,128]{2,1,0:T(4,128)} %copy.231), calls=%async_computation.5 | async-start | bytes 131072 | tf_op jit(solution)/shard_map/all_to_all | solution.py:125
  214.6 8.2 %all-to-all-done.5 = f32[32,3,128]{2,1,0:T(4,128)S(1)} async-done(((f32[32,3,128]{2,1,0:T(4,128)}), f32[32,3,128]{2,1,0:T(4,128)S(1)}, u32[]{:S(2)}, u32[]{:S(2)}) %all-to-all-start.5) | async-done | bytes 49184 | tf_op jit(solution)/shard_map/all_to_all | solution.py:125
  222.8 3.3 %all-to-all-start.4 = ((f32[4,32,128]{2,1,0:T(8,128)}), f32[4,32,128]{2,1,0:T(8,128)S(1)}, u32[]{:S(2)}, u32[]{:S(2)}) async-start(f32[4,32,128]{2,1,0:T(8,128)} %fusion.49), calls=%async_computation.4 | async-start | bytes 131072 | tf_op jit(solution)/shard_map/all_to_all | solution.py:122
  226.2 4.4 %all-to-all-done.4 = f32[4,32,128]{2,1,0:T(8,128)S(1)} async-done(((f32[4,32,128]{2,1,0:T(8,128)}), f32[4,32,128]{2,1,0:T(8,128)S(1)}, u32[]{:S(2)}, u32[]{:S(2)}) %all-to-all-start.4) | async-done | bytes 65568 | tf_op jit(solution)/shard_map/all_to_all | solution.py:122
  230.6 18.7 %all_to_all.36 = f32[8,152,128]{2,1,0:T(8,128)S(1)} all-to-all(f32[8,152,128]{2,1,0:T(8,128)S(1)} %broadcast_in_dim.34), channel_id=1, replica_groups=mesh['y'=8,'core'=2,'x'=4,'z'=8] {'y'}, dimensions={0} | all-to-all | bytes 1245184 | tf_op jit(solution)/shard_map/all_to_all | solution.py:130
  249.4 6.2 %collective-permute-start.5 = (f32[8,152,128]{2,1,0:T(8,128)S(1)}, f32[8,152,128]{2,1,0:T(8,128)S(1)}, u32[]{:S(2)}, u32[]{:S(2)}) collective-permute-start(f32[8,152,128]{2,1,0:T(8,128)S(1)} %all_to_all.36), channel_id=1, source_target_pairs={{0,32},{32,0},{1,33},{33,1},{2,34},{34,2},{3,35},{35,3},{4,36},{36... | collective-permute-start | bytes 1867784 | tf_op jit(solution)/shard_map/ppermute | solution.py:42
  (89 shorter events, 26.4 us)
Async XLA Ops:
  16.3 11.9 %copy-start.4 = (bf16[2,2048,128]{2,1,0:T(8,128)(2,1)S(1)}, bf16[2,2048,128]{2,1,0:T(8,128)(2,1)}, u32[]{:S(2)}) copy-start(bf16[2,2048,128]{2,1,0:T(8,128)(2,1)} %param.9) | copy-start | bytes 3145732
  16.3 17.3 %copy-start.12 = (s32[2,2048,4]{1,2,0:T(4,128)S(1)}, s32[2,2048,4]{1,2,0:T(4,128)}, u32[]{:S(2)}) copy-start(s32[2,2048,4]{1,2,0:T(4,128)} %param.13) | copy-start | bytes 196612
  16.3 108.7 %all-to-all-start.1 = ((bf16[8,512,512]{1,2,0:T(8,128)(2,1)}), bf16[8,512,512]{1,2,0:T(8,128)(2,1)}, u32[]{:S(2)}, u32[]{:S(2)}) async-start(bf16[8,512,512]{1,2,0:T(8,128)(2,1)} %stack.34), calls=%async_computation.1 | async-start | bytes 8388608 | tf_op jit(solution)/shard_map/all_to_all | solution.py:15
  28.1 32.4 %copy-start.8 = (s32[32,4,12]{0,1,2:T(4,128)S(1)}, s32[32,4,12]{0,1,2:T(4,128)}, u32[]{:S(2)}) copy-start(s32[32,4,12]{0,1,2:T(4,128)} %param.14) | copy-start | bytes 18436
  28.2 24.6 %collective-permute-start = (bf16[4096,128]{1,0:T(8,128)(2,1)S(1)}, bf16[4096,128]{1,0:T(8,128)(2,1)S(1)}, u32[]{:S(2)}, u32[]{:S(2)}) collective-permute-start(bf16[4096,128]{1,0:T(8,128)(2,1)S(1)} %bitcast.177), channel_id=1, source_target_pairs={{0,24},{8,0},{16,8},{24,16},{1,25},{9,1},{17,9},{25,17},{2,26},{10... | collective-permute-start | bytes 3145736 | tf_op jit(solution)/shard_map/ppermute | solution.py:42
  31.0 26.7 %collective-permute-start.1 = (bf16[4096,128]{1,0:T(8,128)(2,1)S(1)}, bf16[4096,128]{1,0:T(8,128)(2,1)S(1)}, u32[]{:S(2)}, u32[]{:S(2)}) collective-permute-start(bf16[4096,128]{1,0:T(8,128)(2,1)S(1)} %bitcast.178), channel_id=1, source_target_pairs={{0,8},{8,16},{16,24},{24,0},{1,9},{9,17},{17,25},{25,1},{2,10},{10... | collective-permute-start | bytes 3145736 | tf_op jit(solution)/shard_map/ppermute | solution.py:42
  53.7 18.6 %collective-permute-start.3 = (bf16[2048,128]{1,0:T(8,128)(2,1)}, bf16[2048,128]{1,0:T(8,128)(2,1)}, u32[]{:S(2)}, u32[]{:S(2)}) collective-permute-start(bf16[2048,128]{1,0:T(8,128)(2,1)} %slice.91), channel_id=1, source_target_pairs={{0,24},{8,0},{16,8},{24,16},{1,25},{9,1},{17,9},{25,17},{2,26},{10... | collective-permute-start | bytes 1572872 | tf_op jit(solution)/shard_map/ppermute | solution.py:42
  58.6 13.8 %collective-permute-start.2 = (bf16[2048,128]{1,0:T(8,128)(2,1)}, bf16[2048,128]{1,0:T(8,128)(2,1)}, u32[]{:S(2)}, u32[]{:S(2)}) collective-permute-start(bf16[2048,128]{1,0:T(8,128)(2,1)} %slice.90), channel_id=1, source_target_pairs={{0,8},{8,16},{16,24},{24,0},{1,9},{9,17},{17,25},{25,1},{2,10},{10... | collective-permute-start | bytes 1572872 | tf_op jit(solution)/shard_map/ppermute | solution.py:42
  124.9 39.8 %all-to-all-start.2 = ((bf16[4,128,512]{1,2,0:T(8,128)(2,1)}), bf16[4,128,512]{1,2,0:T(8,128)(2,1)S(1)}, u32[]{:S(2)}, u32[]{:S(2)}) async-start(bf16[4,128,512]{1,2,0:T(8,128)(2,1)} %bitcast.36), calls=%async_computation.2 | async-start | bytes 1048576 | tf_op jit(solution)/shard_map/all_to_all | solution.py:76
  134.9 6.5 %copy-start.6 = (bf16[128,4096]{1,0:T(8,128)(2,1)S(1)}, bf16[128,4096]{1,0:T(8,128)(2,1)}, u32[]{:S(2)}) copy-start(bf16[128,4096]{1,0:T(8,128)(2,1)} %copy.217) | copy-start | bytes 3145732
  141.4 3.8 %copy-start.1 = (bf16[512,4096]{1,0:T(8,128)(2,1)S(1)}, bf16[512,4096]{1,0:T(8,128)(2,1)}, u32[]{:S(2)}) copy-start(bf16[512,4096]{1,0:T(8,128)(2,1)} %copy.214) | copy-start | bytes 12582916
  141.5 3.9 %copy-start.7 = (bf16[128,4096]{1,0:T(8,128)(2,1)S(1)}, bf16[128,4096]{1,0:T(8,128)(2,1)}, u32[]{:S(2)}) copy-start(bf16[128,4096]{1,0:T(8,128)(2,1)} %copy.216) | copy-start | bytes 3145732
  146.8 1.5 copy-start.5
  149.8 2.2 copy-start
  164.8 3.5 %copy-start.3 = (f32[384,512]{1,0:T(8,128)S(1)}, f32[384,512]{1,0:T(8,128)}, u32[]{:S(2)}) copy-start(f32[384,512]{1,0:T(8,128)} %fusion) | copy-start | bytes 2359300
  164.8 3.7 %copy-start.2 = (f32[384,512]{1,0:T(8,128)S(1)}, f32[384,512]{1,0:T(8,128)}, u32[]{:S(2)}) copy-start(f32[384,512]{1,0:T(8,128)} %fusion.2) | copy-start | bytes 2359300
  169.5 4.5 %collective-permute-start.4 = (f32[8,224,128]{2,1,0:T(8,128)S(1)}, f32[8,224,128]{2,1,0:T(8,128)S(1)}, u32[]{:S(2)}, u32[]{:S(2)}) collective-permute-start(f32[8,224,128]{2,1,0:T(8,128)S(1)} %select_bitcast_fusion), channel_id=1, source_target_pairs={{0,32},{32,0},{1,33},{33,1},{2,34},{34,2},{3,35},{35,3},{4,36},{36... | collective-permute-start | bytes 2752520 | tf_op jit(solution)/shard_map/ppermute | solution.py:42
  175.1 33.2 %all-to-all-start.3 = ((f32[8,224,128]{2,1,0:T(8,128)}), f32[8,224,128]{2,1,0:T(8,128)S(1)}, u32[]{:S(2)}, u32[]{:S(2)}) async-start(f32[8,224,128]{2,1,0:T(8,128)} %fusion.34), calls=%async_computation.3 | async-start | bytes 1835008 | tf_op jit(solution)/shard_map/all_to_all | solution.py:116
  209.1 13.7 %all-to-all-start.5 = ((f32[32,3,128]{2,1,0:T(4,128)}), f32[32,3,128]{2,1,0:T(4,128)S(1)}, u32[]{:S(2)}, u32[]{:S(2)}) async-start(f32[32,3,128]{2,1,0:T(4,128)} %copy.231), calls=%async_computation.5 | async-start | bytes 131072 | tf_op jit(solution)/shard_map/all_to_all | solution.py:125
  222.8 7.7 %all-to-all-start.4 = ((f32[4,32,128]{2,1,0:T(8,128)}), f32[4,32,128]{2,1,0:T(8,128)S(1)}, u32[]{:S(2)}, u32[]{:S(2)}) async-start(f32[4,32,128]{2,1,0:T(8,128)} %fusion.49), calls=%async_computation.4 | async-start | bytes 131072 | tf_op jit(solution)/shard_map/all_to_all | solution.py:122
  249.4 9.2 %copy-start.9 = (f32[1,4,12,1024]{3,1,2,0:T(4,128)S(1)}, f32[1,4,12,1024]{3,1,2,0:T(4,128)}, u32[]{:S(2)}) copy-start(f32[1,4,12,1024]{3,1,2,0:T(4,128)} %param.17) | copy-start | bytes 589828
  249.4 9.2 %copy-start.10 = (f32[1,4,12,1024]{3,1,2,0:T(4,128)S(1)}, f32[1,4,12,1024]{3,1,2,0:T(4,128)}, u32[]{:S(2)}) copy-start(f32[1,4,12,1024]{3,1,2,0:T(4,128)} %param.16) | copy-start | bytes 589828
  249.4 9.2 %copy-start.11 = (f32[1,4,12,1024]{3,1,2,0:T(4,128)S(1)}, f32[1,4,12,1024]{3,1,2,0:T(4,128)}, u32[]{:S(2)}) copy-start(f32[1,4,12,1024]{3,1,2,0:T(4,128)} %param.15) | copy-start | bytes 589828
  249.4 7.9 %collective-permute-start.5 = (f32[8,152,128]{2,1,0:T(8,128)S(1)}, f32[8,152,128]{2,1,0:T(8,128)S(1)}, u32[]{:S(2)}, u32[]{:S(2)}) collective-permute-start(f32[8,152,128]{2,1,0:T(8,128)S(1)} %all_to_all.36), channel_id=1, source_target_pairs={{0,32},{32,0},{1,33},{33,1},{2,34},{34,2},{3,35},{35,3},{4,36},{36... | collective-permute-start | bytes 1867784 | tf_op jit(solution)/shard_map/ppermute | solution.py:42
